TPU v7x, 256 devices: a whole 4x4x8 slice. The times are simulated.
256 devices in a mesh: pipe: 16 (over x, z_hi, core), dp: 4 (over z_lo), mp: 4 (over y).
Axes of the slice: x: 4, y: 4, z: 8 (z_hi: 2, z_lo: 4; z = z_hi * 4 + z_lo), core: 2. Of those that a mesh axis runs over, the one named last changes fastest.
Arguments:
- layer_input: bfloat16 [16, 1024, 16384], P('pipe', 'dp', 'mp'), may hold values from -6 to 6
- kv_cotangent: bfloat16 [16, 1024, 2, 1024], P('pipe', 'dp', None, 'mp'), may hold values from -6 to 6
- kv_weight: bfloat16 [16, 16384, 2, 1024], P('pipe', 'dp', None, 'mp'), may hold values from -0.046875 to 0.046875
Outputs:
- input_grad: bfloat16 [16, 1024, 16384], P('pipe', None, ('dp', 'mp'))
- grad_mantissa: bfloat16 [16, 16384, 2, 1024], P('pipe', 'dp', None, 'mp')
- grad_scale: float32 [16, 16384, 2, 8], P('pipe', 'dp', None, 'mp')
All inputs are finite; a program needn't handle non-finite values. Where the computation divides by a largest or mean magnitude, that divisor is 1e-20 or more.
Results may differ from a plain program's by a relative error of at most 0.018.
Values may be sent and summed in bfloat16 or wider, within the bound.
A program may use at most 192 MiB of HBM per device.

v0:
```python
import jax
import jax.numpy as jnp
from jax import lax
from jax.sharding import PartitionSpec as P

BLOCK = 128


def passed_along(x, axis, by):
    devices = lax.axis_size(axis)
    pairs = [(i, i + by) for i in range(devices) if 0 <= i + by < devices]
    return lax.ppermute(x, axis, pairs)


def on_device(layer_input, kv_cotangent, kv_weight):
    features = layer_input[0]
    grads = kv_cotangent[0]
    weights = kv_weight[0]
    row_count = grads.shape[0]
    columns = 2 * grads.shape[2]
    flat_grad = grads.reshape(row_count, columns)
    flat_weight = weights.reshape(weights.shape[0], columns)
    weight_grad = lax.dot_general(
        lax.all_gather(features, "mp", axis=1, tiled=True),
        flat_grad,
        (((0,), (0,)), ((), ())),
        preferred_element_type=jnp.float32,
    )
    piece = lax.all_gather(grads, "dp", axis=0, tiled=True)
    flat_piece = piece.reshape(piece.shape[0], columns)
    partial_sum = lax.dot_general(
        flat_piece, flat_weight, (((1,), (1,)), ((), ())), preferred_element_type=jnp.float32
    )
    summed = lax.psum_scatter(
        partial_sum.astype(jnp.bfloat16), "mp", scatter_dimension=1, tiled=True
    )
    arrived = passed_along(summed, "pipe", -1)
    row_total = weight_grad.shape[0]
    blocked = weight_grad.reshape(row_total, columns // BLOCK, BLOCK)
    local_max = jnp.max(jnp.abs(blocked), axis=2)
    block_scale = lax.pmax(local_max.astype(jnp.bfloat16), "dp").astype(local_max.dtype) + 1e-06
    scaled = (blocked / block_scale[:, :, None]).astype(jnp.bfloat16).astype(jnp.float32)
    totals = lax.psum_scatter(
        scaled.reshape(row_total, columns).astype(jnp.bfloat16),
        "dp",
        scatter_dimension=0,
        tiled=True,
    ).astype(jnp.float32)
    share = totals.shape[0]
    mantissa = totals.astype(jnp.bfloat16).reshape(share, 2, columns // 2)
    own_scale = lax.dynamic_slice_in_dim(block_scale, lax.axis_index("dp") * share, share, 0)
    own_scale = own_scale.reshape(share, 2, columns // (2 * BLOCK))
    return (arrived[None], mantissa[None], own_scale[None])


def solution(mesh):
    in_specs = (P("pipe", "dp", "mp"), P("pipe", "dp", None, "mp"), P("pipe", "dp", None, "mp"))
    out_specs = (
        P("pipe", None, ("dp", "mp")),
        P("pipe", "dp", None, "mp"),
        P("pipe", "dp", None, "mp"),
    )
    return jax.shard_map(
        on_device, mesh=mesh, in_specs=in_specs, out_specs=out_specs, check_vma=False
    )
```

profile of v0, /device:TPU:2, one launch (start us, length us, event | category | flops | bytes accessed | tf_op | source)
XLA Modules:
  0.0 628.9 jit_solution(4210856352971520837)
XLA Ops:
  7.2 0.7 all-gather.5.cloned.1.call-update
  7.9 0.0 all-gather.7.cloned.1.call-start
  7.9 0.7 all-gather.7.cloned.1.call-update
  8.6 0.0 all-reduce.2.cloned.1.call-start
  8.7 1.0 copy.14
  9.7 0.1 copy.9
  9.8 4.9 copy.13
  14.8 31.6 %all-gather.5.cloned.1.call-done = bf16[1,1024,2,256]{3,2,0,1:T(2,128)(2,1)} async-done(((bf16[1,256,2,256]{3,2,0,1:T(2,128)(2,1)}), bf16[1,1024,2,256]{3,2,0,1:T(2,128)(2,1)}) %all-gather.5.cloned.1.call-update) | async-done | bytes 1048592 | tf_op jit(solution)/shard_map/all_gather | solution.py:29
  46.3 1.4 copy.12
  47.8 85.1 %all-gather.7.cloned.1.call-done = bf16[1,256,16384]{2,1,0:T(8,128)(2,1)} async-done(((bf16[1,256,4096]{2,1,0:T(8,128)(2,1)}), bf16[1,256,16384]{2,1,0:T(8,128)(2,1)}) %all-gather.7.cloned.1.call-update) | async-done | bytes 8388624 | tf_op jit(solution)/shard_map/all_gather | solution.py:24
  132.8 17.3 %abs_reduce_fusion = (bf16[16384,4]{0,1:T(4,128)(2,1)}, f32[16384,4,128]{0,2,1:T(8,128)}) fusion(bf16[4,128,256]{2,1,0:T(8,128)(2,1)S(1)} %bitcast.33, bf16[1,256,16384]{2,1,0:T(8,128)(2,1)} %all-gather.7.cloned.1.call-done), kind=kOutput, calls=%fused_computation.1 | convolution fusion | flops 4320067584 | bytes 42336256 | tf_op jit(solution)/shard_map/dot_general | solution.py:23
  150.1 0.0 reduce-scatter.3.cloned.1.call-start
  150.2 8.9 %convolution_convert_fusion = bf16[1024,4096]{1,0:T(8,128)(2,1)} fusion(bf16[1024,512]{1,0:T(8,128)(2,1)S(1)} %bitcast.35, bf16[4096,512]{1,0:T(8,128)(2,1)} %bitcast.31), kind=kOutput, calls=%fused_computation.4 | convolution fusion | flops 4299161600 | bytes 13631488 | tf_op jit(solution)/shard_map/dot_general | solution.py:31
  159.2 0.0 reduce-scatter.5.cloned.1.call-start
  159.2 40.7 %all-reduce.2.cloned.1.call-done = bf16[16384,4]{0,1:T(4,128)(2,1)} async-done(((bf16[16384,4]{0,1:T(4,128)(2,1)}), bf16[16384,4]{0,1:T(4,128)(2,1)}) %all-reduce.2.cloned.1.call-update) | async-done | bytes 131088 | tf_op jit(solution)/shard_map/pmax | solution.py:41
  199.9 1.0 convert_add_fusion
  200.9 18.2 %divide_convert_fusion = bf16[16384,4,128]{0,2,1:T(8,128)(2,1)} fusion(f32[16384,4,128]{0,2,1:T(8,128)} %get-tuple-element.4, f32[16384,4]{0,1:T(4,128)S(1)} %convert_add_fusion), kind=kLoop, calls=%fused_computation | loop fusion | flops 16777216 | bytes 50593792 | tf_op jit(solution)/shard_map/convert_element_type | solution.py:42
  219.1 65.1 %reduce-scatter.3.cloned.1.call-done = bf16[1024,1024]{1,0:T(8,128)(2,1)} async-done(((bf16[1024,4096]{1,0:T(8,128)(2,1)}), bf16[1024,1024]{1,0:T(8,128)(2,1)}) %reduce-scatter.3.cloned.1.call-update) | async-done | bytes 2097168 | tf_op jit(solution)/shard_map/reduce_scatter | solution.py:34
  284.3 7.1 %collective-permute-start = (bf16[1024,1024]{1,0:T(8,128)(2,1)}, bf16[1024,1024]{1,0:T(8,128)(2,1)S(1)}, u32[]{:S(2)}, u32[]{:S(2)}) collective-permute-start(bf16[1024,1024]{1,0:T(8,128)(2,1)} %reduce-scatter.3.cloned.1.call-done), channel_id=1, source_target_pairs={{16,0},{32,16},{48,32},{64,48},{80,64},{96,80},{112,96},{128,112},... | collective-permute-start | bytes 6291464 | tf_op jit(solution)/shard_map/ppermute | solution.py:12
  291.4 0.7 broadcast_in_dim_reshape.7
  292.1 73.0 %collective-permute-done = bf16[1024,1024]{1,0:T(8,128)(2,1)S(1)} collective-permute-done((bf16[1024,1024]{1,0:T(8,128)(2,1)}, bf16[1024,1024]{1,0:T(8,128)(2,1)S(1)}, u32[]{:S(2)}, u32[]{:S(2)}) %collective-permute-start) | collective-permute-done | bytes 2097184 | tf_op jit(solution)/shard_map/ppermute | solution.py:12
  365.1 244.8 %reduce-scatter.5.cloned.1.call-done = bf16[4096,512]{0,1:T(8,128)(2,1)} async-done(((bf16[16384,512]{0,1:T(8,128)(2,1)}), bf16[4096,512]{0,1:T(8,128)(2,1)}) %reduce-scatter.5.cloned.1.call-update) | async-done | bytes 4194320 | tf_op jit(solution)/shard_map/reduce_scatter | solution.py:43
  609.9 11.1 %copy.11 = bf16[1,4096,2,256]{3,2,1,0:T(2,128)(2,1)} copy(bf16[1,4096,2,256]{1,3,2,0:T(8,128)(2,1)} %bitcast.30) | data formatting | bytes 8388608 | tf_op jit(solution)/shard_map/broadcast_in_dim;reshape | solution.py:53
  621.0 1.3 copy.17
  (5 shorter events, 0.1 us)
Async XLA Ops:
  7.2 39.1 %all-gather.5.cloned.1.call-start = ((), (), s32[]{:S(2)}) async-start(), calls=%async_computation.5 | async-start | bytes 1310720 | tf_op jit(solution)/shard_map/all_gather | solution.py:29
  7.9 125.0 %all-gather.7.cloned.1.call-start = ((), (), s32[]{:S(2)}) async-start(), calls=%async_computation.6 | async-start | bytes 10485760 | tf_op jit(solution)/shard_map/all_gather | solution.py:24
  8.6 191.3 %all-reduce.2.cloned.1.call-start = ((), (), s32[]{:S(2)}) async-start(), calls=%async_computation.3 | async-start | bytes 262144 | tf_op jit(solution)/shard_map/pmax | solution.py:41
  150.1 134.1 %reduce-scatter.3.cloned.1.call-start = ((), (), s32[]{:S(2)}) async-start(), calls=%async_computation.2 | async-start | bytes 10485760 | tf_op jit(solution)/shard_map/reduce_scatter | solution.py:34
  159.2 450.8 %reduce-scatter.5.cloned.1.call-start = ((), (), s32[]{:S(2)}) async-start(), calls=%async_computation.4 | async-start | bytes 20971520 | tf_op jit(solution)/shard_map/reduce_scatter | solution.py:43
  284.3 80.8 %collective-permute-start = (bf16[1024,1024]{1,0:T(8,128)(2,1)}, bf16[1024,1024]{1,0:T(8,128)(2,1)S(1)}, u32[]{:S(2)}, u32[]{:S(2)}) collective-permute-start(bf16[1024,1024]{1,0:T(8,128)(2,1)} %reduce-scatter.3.cloned.1.call-done), channel_id=1, source_target_pairs={{16,0},{32,16},{48,32},{64,48},{80,64},{96,80},{112,96},{128,112},... | collective-permute-start | bytes 6291464 | tf_op jit(solution)/shard_map/ppermute | solution.py:12
Sparse Core Ops, SparseCore 0:
  9.8 36.4 all-gather.4
  48.1 84.6 all-gather.6
  150.3 49.5 all-reduce.1
  202.6 81.6 reduce-scatter.2
  286.9 322.9 reduce-scatter.4
where the time goes:
time: 630 us; the launch traced here: 629 us
  waiting for transfers between devices  542 us (86%)
  matrix products  26.2 us (4%)
  local copies, waits for them, and re-layouts  20.6 us (3%)
  other arithmetic  19.2 us (3%)
  between operations  13.8 us (2%)
  starting transfers between devices  7.33 us (1%)
    reduce_scatter x1, waiting for transfers between devices, on_device(): lax.psum_scatter(scaled.reshape(row_total, columns).astype(jnp.bfloat16),...  245 us
    all_gather x1, waiting for transfers between devices, on_device(): lax.all_gather(features, 'mp', axis=1, tiled=True)  85.1 us
    ppermute x1, waiting for transfers between devices, passed_along(): return lax.ppermute(x, axis, pairs)  73 us
    reduce_scatter x1, waiting for transfers between devices, on_device(): lax.psum_scatter(partial_sum.astype(jnp.bfloat16), 'mp', scatter_dimensio...  65.1 us
    pmax x1, waiting for transfers between devices, on_device(): lax.pmax(local_max.astype(jnp.bfloat16), 'dp').astype(local_max.dtype)  40.7 us
    all_gather x1, waiting for transfers between devices, on_device(): piece = lax.all_gather(grads, 'dp', axis=0, tiled=True)  31.6 us
    convert_element_type x1, other arithmetic, on_device(): (blocked / block_scale[:, :, None]).astype(jnp.bfloat16).astype(jnp.float32)  18.2 us
    dot_general x1, matrix products, on_device(): lax.dot_general(lax.all_gather(features, 'mp', axis=1, tiled=True), flat_...  17.3 us
  transfers between devices with their start and end apart: 6, of which 6 were waited for; matrix products, arithmetic and copies ran while one was open for 6% of the time, Pallas kernels for 0%

commit v1 on v0

v1 whole, which is shorter than its diff:
```python
import functools

import jax
import jax.numpy as jnp
from jax import lax
from jax.experimental import pallas as pl
from jax.experimental.pallas import tpu as pltpu
from jax.sharding import PartitionSpec as P

BLOCK = 128
TINY = 1e-6
MESH = pl.DeviceIdType.MESH
PARTS = 4


def wrap(index):
    return lax.rem(index + 2 * PARTS, PARTS)


def section_kernel(
    sections,
    x_ref,
    g_ref,
    w_ref,
    out_grad,
    out_mant,
    out_scale,
    x_stage,
    x_all,
    g_all,
    w_all,
    mant,
    scale,
    made,
    zeros,
    x_send,
    x_recv,
    xz_send,
    xz_recv,
    gz_send,
    gz_recv,
    gy_send,
    gy_recv,
    gf_send,
    gf_recv,
    w_send,
    w_recv,
    m_send,
    m_recv,
    s_send,
    s_recv,
    p_send,
    p_recv,
    local_sem,
    m_local,
    zero_sem,
):
    pipe, dp, mp = lax.axis_index("pipe"), lax.axis_index("dp"), lax.axis_index("mp")
    tokens, features = x_ref.shape
    columns = g_ref.shape[1]
    share = features // PARTS
    chunk = share // PARTS
    all_tokens = tokens * PARTS
    half = all_tokens // 2
    blocks = columns // BLOCK

    def along_mp(by):
        return (pipe, dp, wrap(mp + by))

    def along_dp(to):
        return (pipe, to, mp)

    def remote(src, dst, send, recv, device):
        return pltpu.make_async_remote_copy(
            src_ref=src, dst_ref=dst, send_sem=send, recv_sem=recv, device_id=device, device_id_type=MESH
        )

    barrier = pltpu.get_barrier_semaphore()
    for by in range(1, PARTS):
        pl.semaphore_signal(barrier, inc=1, device_id=along_mp(by), device_id_type=MESH)
        pl.semaphore_signal(barrier, inc=1, device_id=along_dp(wrap(dp + by)), device_id_type=MESH)

    for by in (1, sections - 1):
        pl.semaphore_signal(
            barrier, inc=1, device_id=(lax.rem(pipe + by, sections), dp, mp), device_id_type=MESH
        )
    pl.semaphore_wait(barrier, 2 * (PARTS - 1) + 2)

    def quarter(index):
        return pl.ds(pl.multiple_of(index * share, share), share)

    def token_rows(index):
        return pl.ds(pl.multiple_of(index * tokens, tokens), tokens)

    x_out = [
        remote(
            x_ref.at[:, quarter(wrap(mp + by))], x_stage.at[by], x_send.at[by], x_recv.at[by], along_mp(by)
        )
        for by in range(1, PARTS)
    ]
    for copy in x_out:
        copy.start()
    own_g = pltpu.make_async_copy(g_ref, g_all.at[0, token_rows(dp)], local_sem.at[0])
    own_w = pltpu.make_async_copy(w_ref.at[quarter(mp)], w_all.at[0], local_sem.at[1])
    own_g.start()
    gz_out = [
        remote(
            g_ref, g_all.at[0, token_rows(dp)], gz_send.at[by], gz_recv.at[by], along_dp(wrap(dp + by))
        )
        for by in range(1, PARTS)
    ]
    for copy in gz_out:
        copy.start()
    own_w.start()

    def x_from(by):
        return x_ref.at[:, quarter(mp)] if by == 0 else x_stage.at[by]

    def x_on(by):
        owner = wrap(mp - by)
        return remote(x_from(by), x_all.at[dp], xz_send.at[by], xz_recv.at[dp], along_dp(owner))

    for by in range(PARTS):
        if by > 0:
            x_out[by - 1].wait_recv()

        @pl.when(wrap(mp - by) != dp)
        def _():
            x_on(by).start()

        @pl.when(wrap(mp - by) == dp)
        def _():
            pltpu.make_async_copy(x_from(by), x_all.at[dp], local_sem.at[2]).start()

    own_g.wait()
    for by in range(1, PARTS):
        remote(
            g_ref, g_all.at[0, token_rows(wrap(dp - by))], gz_send.at[by], gz_recv.at[by], along_dp(wrap(dp + by))
        ).wait_recv()

    def g_half(slot, part):
        return g_all.at[slot, pl.ds(part * half, half)]

    def g_out(side, part):
        by, slot = (1, 1) if side == 0 else (-1, 3)
        return remote(
            g_half(0, part), g_half(slot, part), gy_send.at[side, part], gy_recv.at[side, part], along_mp(by)
        )

    def g_on(side):
        by, slot = (1, 1) if side == 0 else (-1, 3)
        return remote(g_half(slot, side), g_half(2, side), gf_send.at[side], gf_recv.at[side], along_mp(by))

    for part in range(2):
        g_out(0, part).start()
        g_out(1, 1 - part).start()

    def w_out(by, part):
        rows = pl.ds(pl.multiple_of(wrap(mp + by) * share + part * chunk, chunk), chunk)
        return remote(
            w_ref.at[rows],
            w_all.at[by, pl.ds(pl.multiple_of(part * chunk, chunk), chunk)],
            w_send.at[by, part],
            w_recv.at[by, part],
            along_mp(by),
        )

    for by in range(1, PARTS):
        w_out(by, 0).start()
    for side in range(2):
        g_out(side, side).wait_recv()
        g_on(side).start()
    for part in range(1, PARTS):
        for by in range(1, PARTS):
            w_out(by, part).start()

    @pl.when(pipe == sections - 1)
    def _():
        zeros[...] = jnp.zeros_like(zeros)
        for part in range(PARTS):
            pltpu.make_async_copy(
                zeros, out_grad.at[pl.ds(part * tokens, tokens)], zero_sem.at[part]
            ).start()

    for side in range(2):
        g_out(side, 1 - side).wait_recv()
        g_on(side).wait_recv()
    for by in range(1, PARTS):
        source = wrap(dp - by)
        remote(x_stage.at[0], x_all.at[source], xz_send.at[0], xz_recv.at[source], along_dp(source)).wait_recv()
    pltpu.make_async_copy(x_stage.at[0], x_all.at[dp], local_sem.at[2]).wait()

    def m_out(turn, part):
        rows = pl.ds(pl.multiple_of(mp * share + part * chunk, chunk), chunk)
        src = mant.at[turn, pl.ds(pl.multiple_of(part * chunk, chunk), chunk)]
        return remote(src, out_mant.at[rows], m_send.at[turn, part], m_recv.at[turn, part], along_mp(1 + turn))

    def m_here(part):
        rows = pl.ds(pl.multiple_of(mp * share + part * chunk, chunk), chunk)
        src = mant.at[PARTS - 1, pl.ds(pl.multiple_of(part * chunk, chunk), chunk)]
        return pltpu.make_async_copy(src, out_mant.at[rows], m_local.at[part])

    def weight_step(step, _):
        turn, part = step // PARTS, lax.rem(step, PARTS)
        slot = PARTS - 1 - turn
        rows = pl.ds(pl.multiple_of(part * chunk, chunk), chunk)
        partial = [
            lax.dot_general(
                x_all[group, :, rows],
                g_all[slot, pl.ds(group * tokens, tokens), :],
                (((0,), (0,)), ((), ())),
                preferred_element_type=jnp.float32,
            )
            for group in range(PARTS)
        ]
        largest = jnp.abs(partial[0])
        for group in range(1, PARTS):
            largest = jnp.maximum(largest, jnp.abs(partial[group]))
        lanes = lax.broadcasted_iota(jnp.int32, (chunk, BLOCK), 1)
        gathered = jnp.zeros((chunk, BLOCK), jnp.float32)
        for block in range(blocks):
            cols = slice(block * BLOCK, (block + 1) * BLOCK)
            size = jnp.max(largest[:, cols], axis=1, keepdims=True) + TINY
            gathered = jnp.where(lanes == block, size, gathered)
            inverse = 1.0 / size
            total = None
            for group in range(PARTS):
                term = (partial[group][:, cols] * inverse).astype(jnp.bfloat16).astype(jnp.float32)
                total = term if total is None else total + term
            mant[turn, rows, cols] = total.astype(jnp.bfloat16)
        scale[turn, :, rows] = jnp.transpose(gathered)[:8, :]

        @pl.when(turn < PARTS - 1)
        def _():
            m_out(turn, part).start()

        @pl.when(turn == PARTS - 1)
        def _():
            m_here(part).start()

        return 0

    lax.fori_loop(0, PARTS * PARTS, weight_step, 0)

    def s_out(turn):
        cols = pl.ds(pl.multiple_of(mp * share, share), share)
        return remote(scale.at[turn], out_scale.at[:, cols], s_send.at[turn], s_recv.at[turn], along_mp(1 + turn))

    for turn in range(PARTS - 1):
        s_out(turn).start()
    s_here = pltpu.make_async_copy(
        scale.at[PARTS - 1], out_scale.at[:, pl.ds(pl.multiple_of(mp * share, share), share)], local_sem.at[3]
    )
    s_here.start()

    def p_out(part):
        cols = pl.ds(pl.multiple_of(part * chunk, chunk), chunk)
        before = jnp.maximum(pipe - 1, 0)
        return remote(
            made.at[:, cols], out_grad.at[:, cols], p_send.at[part], p_recv.at[part], (before, dp, mp)
        )

    own_w.wait()

    def input_step(part, _):
        for by in range(1, PARTS):
            w_out(by, part).wait_recv()
        rows = pl.ds(pl.multiple_of(part * chunk, chunk), chunk)

        def token_step(group, _):
            own = pl.ds(pl.multiple_of(group * tokens, tokens), tokens)
            total = None
            for slot in range(PARTS):
                term = lax.dot_general(
                    g_all[slot, own, :],
                    w_all[slot, rows, :],
                    (((1,), (1,)), ((), ())),
                    preferred_element_type=jnp.float32,
                )
                total = term if total is None else total + term
            made[own, rows] = total.astype(jnp.bfloat16)
            return 0

        lax.fori_loop(0, PARTS, token_step, 0)

        @pl.when(pipe > 0)
        def _():
            p_out(part).start()

        return 0

    lax.fori_loop(0, PARTS, input_step, 0)

    for copy in x_out + gz_out:
        copy.wait_send()
    for by in range(PARTS):

        @pl.when(wrap(mp - by) != dp)
        def _():
            x_on(by).wait_send()

    for side in range(2):
        for part in range(2):
            g_out(side, part).wait_send()
        g_on(side).wait_send()
    for by in range(1, PARTS):
        for part in range(PARTS):
            w_out(by, part).wait_send()
    for turn in range(PARTS - 1):
        source = wrap(mp - 1 - turn)
        for part in range(PARTS):
            m_out(turn, part).wait_send()
            rows = pl.ds(pl.multiple_of(source * share + part * chunk, chunk), chunk)
            remote(
                mant.at[turn, pl.ds(part * chunk, chunk)],
                out_mant.at[rows],
                m_send.at[turn, part],
                m_recv.at[turn, part],
                along_mp(1 + turn),
            ).wait_recv()
        s_out(turn).wait_send()
        cols = pl.ds(pl.multiple_of(source * share, share), share)
        remote(
            scale.at[turn], out_scale.at[:, cols], s_send.at[turn], s_recv.at[turn], along_mp(1 + turn)
        ).wait_recv()
    for part in range(PARTS):
        m_here(part).wait()
    s_here.wait()

    @pl.when(pipe > 0)
    def _():
        for part in range(PARTS):
            p_out(part).wait_send()

    @pl.when(pipe < sections - 1)
    def _():
        for part in range(PARTS):
            p_out(part).wait_recv()

    @pl.when(pipe == sections - 1)
    def _():
        for part in range(PARTS):
            pltpu.make_async_copy(
                zeros, out_grad.at[pl.ds(part * tokens, tokens)], zero_sem.at[part]
            ).wait()


def on_device(sections, layer_input, kv_cotangent, kv_weight):
    features = layer_input[0]
    tokens, width = features.shape
    columns = 2 * kv_cotangent.shape[3]
    rows = kv_weight.shape[1]
    flat_grad = kv_cotangent.reshape(tokens, columns)
    flat_weight = kv_weight.reshape(rows, columns)
    share = width // PARTS
    blocks = columns // BLOCK
    dma = pltpu.SemaphoreType.DMA
    anywhere = pl.BlockSpec(memory_space=pl.ANY)
    grad, mantissa, scale = pl.pallas_call(
        functools.partial(section_kernel, sections),
        out_shape=(
            jax.ShapeDtypeStruct((tokens * PARTS, share), jnp.bfloat16),
            jax.ShapeDtypeStruct((rows, columns), jnp.bfloat16),
            jax.ShapeDtypeStruct((8, rows), jnp.float32),
        ),
        in_specs=[anywhere] * 3,
        out_specs=[anywhere] * 3,
        scratch_shapes=[
            pltpu.VMEM((PARTS, tokens, share), jnp.bfloat16),
            pltpu.VMEM((PARTS, tokens, share), jnp.bfloat16),
            pltpu.VMEM((PARTS, tokens * PARTS, columns), jnp.bfloat16),
            pltpu.VMEM((PARTS, share, columns), jnp.bfloat16),
            pltpu.VMEM((PARTS, share, columns), jnp.bfloat16),
            pltpu.VMEM((PARTS, 8, share), jnp.float32),
            pltpu.VMEM((tokens * PARTS, share), jnp.bfloat16),
            pltpu.VMEM((tokens, share), jnp.bfloat16),
            dma((PARTS,)),
            dma((PARTS,)),
            dma((PARTS,)),
            dma((PARTS,)),
            dma((PARTS,)),
            dma((PARTS,)),
            dma((2, 2)),
            dma((2, 2)),
            dma((2,)),
            dma((2,)),
            dma((PARTS, PARTS)),
            dma((PARTS, PARTS)),
            dma((PARTS, PARTS)),
            dma((PARTS, PARTS)),
            dma((PARTS,)),
            dma((PARTS,)),
            dma((PARTS,)),
            dma((PARTS,)),
            dma((4,)),
            dma((PARTS,)),
            dma((PARTS,)),
        ],
        name="section",
        compiler_params=pltpu.CompilerParams(
            collective_id=0, has_side_effects=True, vmem_limit_bytes=48 << 20
        ),
    )(features, flat_grad, flat_weight)
    mantissa = mantissa.reshape(rows, 2, columns // 2)
    scale = scale[:blocks].T.reshape(rows, 2, blocks // 2)
    return grad[None], mantissa[None], scale[None]


def solution(mesh):
    in_specs = (P("pipe", "dp", "mp"), P("pipe", "dp", None, "mp"), P("pipe", "dp", None, "mp"))
    out_specs = (
        P("pipe", None, ("dp", "mp")),
        P("pipe", "dp", None, "mp"),
        P("pipe", "dp", None, "mp"),
    )
    return jax.shard_map(
        functools.partial(on_device, mesh.shape["pipe"]),
        mesh=mesh,
        in_specs=in_specs,
        out_specs=out_specs,
        check_vma=False,
    )
```

time: 630 us -> 207 us (0.33)
  the two profiles are of different devices: /device:TPU:2 before, /device:TPU:106 now
where the time goes in v1:
time: 207 us
  Pallas kernels  192 us (93%)
  local copies, waits for them, and re-layouts  15 us (7%)
    pallas_call x1, Pallas kernels, on_device(): pl.pallas_call(functools.partial(section_kernel, sections), out_shape=(ja...  192 us
    another operation x2, local copies, waits for them, and re-layouts, on_device(): return (grad[None], mantissa[None], scale[None])  7.57 us
    unnamed x5, local copies, waits for them, and re-layouts  7.39 us

profile of v1, /device:TPU:106, one launch (start us, length us, event | category | flops | bytes accessed | tf_op | source)
XLA Modules:
  0.0 207.2 jit_solution(10020932822606716300)
XLA Ops:
  0.6 1.0 copy.6
  1.6 0.0 copy-start
  1.6 5.1 %copy.7 = bf16[512,8,2,256]{3,1,2,0:T(8,128)(2,1)} copy(bf16[512,8,2,256]{3,2,1,0:T(2,128)(2,1)} %bitcast.16) | data formatting | bytes 8388608
  6.7 0.0 copy-done
  6.7 191.6 %section.1 = (bf16[1024,1024]{1,0:T(8,128)(2,1)S(1)}, bf16[4096,512]{1,0:T(8,128)(2,1)}, f32[8,4096]{1,0:T(8,128)S(1)}) custom-call(bf16[256,4096]{1,0:T(8,128)(2,1)S(1)} %bitcast.12, bf16[256,512]{1,0:T(8,128)(2,1)S(1)} %bitcast.14, bf16[4096,512]{1,0:T(8,128)(2,1)} %bitcast.15), custom_call_target="tpu_custom_call" | custom-call | tf_op jit(solution)/shard_map/section/pallas_call | solution.py:359
  198.3 0.7 broadcast_in_dim_reshape.7
  199.0 6.9 %broadcast_in_dim_reshape.6 = bf16[1,4096,2,256]{3,2,1,0:T(2,128)(2,1)} reshape(bf16[4096,512]{1,0:T(8,128)(2,1)} %get-tuple-element.7) | data formatting | bytes 8388608 | tf_op jit(solution)/shard_map/broadcast_in_dim;reshape | solution.py:406
  205.9 1.3 copy.9
  (1 shorter events, 0.0 us)
Async XLA Ops:
  1.6 5.1 %copy-start = (bf16[1,256,4096]{2,1,0:T(8,128)(2,1)S(1)}, bf16[1,256,4096]{2,1,0:T(8,128)(2,1)}, u32[]{:S(2)}) copy-start(bf16[1,256,4096]{2,1,0:T(8,128)(2,1)} %param.3) | copy-start | bytes 6291460

commit v2 on v1

--- a/solution.py
+++ b/solution.py
@@ -132,29 +132,6 @@
         def _():
             pltpu.make_async_copy(x_from(by), x_all.at[dp], local_sem.at[2]).start()
 
-    own_g.wait()
-    for by in range(1, PARTS):
-        remote(
-            g_ref, g_all.at[0, token_rows(wrap(dp - by))], gz_send.at[by], gz_recv.at[by], along_dp(wrap(dp + by))
-        ).wait_recv()
-
-    def g_half(slot, part):
-        return g_all.at[slot, pl.ds(part * half, half)]
-
-    def g_out(side, part):
-        by, slot = (1, 1) if side == 0 else (-1, 3)
-        return remote(
-            g_half(0, part), g_half(slot, part), gy_send.at[side, part], gy_recv.at[side, part], along_mp(by)
-        )
-
-    def g_on(side):
-        by, slot = (1, 1) if side == 0 else (-1, 3)
-        return remote(g_half(slot, side), g_half(2, side), gf_send.at[side], gf_recv.at[side], along_mp(by))
-
-    for part in range(2):
-        g_out(0, part).start()
-        g_out(1, 1 - part).start()
-
     def w_out(by, part):
         rows = pl.ds(pl.multiple_of(wrap(mp + by) * share + part * chunk, chunk), chunk)
         return remote(
@@ -165,12 +142,37 @@
             along_mp(by),
         )
 
+    for part in range(PARTS // 2):
+        for by in range(1, PARTS):
+            w_out(by, part).start()
+
+    own_g.wait()
     for by in range(1, PARTS):
-        w_out(by, 0).start()
+        remote(
+            g_ref, g_all.at[0, token_rows(wrap(dp - by))], gz_send.at[by], gz_recv.at[by], along_dp(wrap(dp + by))
+        ).wait_recv()
+
+    def g_half(slot, part):
+        return g_all.at[slot, pl.ds(part * half, half)]
+
+    def g_out(side, part):
+        by, slot = (1, 1) if side == 0 else (-1, 3)
+        return remote(
+            g_half(0, part), g_half(slot, part), gy_send.at[side, part], gy_recv.at[side, part], along_mp(by)
+        )
+
+    def g_on(side):
+        by, slot = (1, 1) if side == 0 else (-1, 3)
+        return remote(g_half(slot, side), g_half(2, side), gf_send.at[side], gf_recv.at[side], along_mp(by))
+
+    for part in range(2):
+        g_out(0, part).start()
+        g_out(1, 1 - part).start()
+
     for side in range(2):
         g_out(side, side).wait_recv()
         g_on(side).start()
-    for part in range(1, PARTS):
+    for part in range(PARTS // 2, PARTS):
         for by in range(1, PARTS):
             w_out(by, part).start()
 
@@ -185,6 +187,44 @@
     for side in range(2):
         g_out(side, 1 - side).wait_recv()
         g_on(side).wait_recv()
+    def p_out(part):
+        cols = pl.ds(pl.multiple_of(part * chunk, chunk), chunk)
+        before = jnp.maximum(pipe - 1, 0)
+        return remote(
+            made.at[:, cols], out_grad.at[:, cols], p_send.at[part], p_recv.at[part], (before, dp, mp)
+        )
+
+    own_w.wait()
+
+    def input_step(part, _):
+        for by in range(1, PARTS):
+            w_out(by, part).wait_recv()
+        rows = pl.ds(pl.multiple_of(part * chunk, chunk), chunk)
+
+        def token_step(group, _):
+            own = pl.ds(pl.multiple_of(group * tokens, tokens), tokens)
+            total = None
+            for slot in range(PARTS):
+                term = lax.dot_general(
+                    g_all[slot, own, :],
+                    w_all[slot, rows, :],
+                    (((1,), (1,)), ((), ())),
+                    preferred_element_type=jnp.float32,
+                )
+                total = term if total is None else total + term
+            made[own, rows] = total.astype(jnp.bfloat16)
+            return 0
+
+        lax.fori_loop(0, PARTS, token_step, 0)
+
+        @pl.when(pipe > 0)
+        def _():
+            p_out(part).start()
+
+        return 0
+
+    lax.fori_loop(0, PARTS // 2, input_step, 0)
+
     for by in range(1, PARTS):
         source = wrap(dp - by)
         remote(x_stage.at[0], x_all.at[source], xz_send.at[0], xz_recv.at[source], along_dp(source)).wait_recv()
@@ -253,43 +293,7 @@
     )
     s_here.start()
 
-    def p_out(part):
-        cols = pl.ds(pl.multiple_of(part * chunk, chunk), chunk)
-        before = jnp.maximum(pipe - 1, 0)
-        return remote(
-            made.at[:, cols], out_grad.at[:, cols], p_send.at[part], p_recv.at[part], (before, dp, mp)
-        )
-
-    own_w.wait()
-
-    def input_step(part, _):
-        for by in range(1, PARTS):
-            w_out(by, part).wait_recv()
-        rows = pl.ds(pl.multiple_of(part * chunk, chunk), chunk)
-
-        def token_step(group, _):
-            own = pl.ds(pl.multiple_of(group * tokens, tokens), tokens)
-            total = None
-            for slot in range(PARTS):
-                term = lax.dot_general(
-                    g_all[slot, own, :],
-                    w_all[slot, rows, :],
-                    (((1,), (1,)), ((), ())),
-                    preferred_element_type=jnp.float32,
-                )
-                total = term if total is None else total + term
-            made[own, rows] = total.astype(jnp.bfloat16)
-            return 0
-
-        lax.fori_loop(0, PARTS, token_step, 0)
-
-        @pl.when(pipe > 0)
-        def _():
-            p_out(part).start()
-
-        return 0
-
-    lax.fori_loop(0, PARTS, input_step, 0)
+    lax.fori_loop(PARTS // 2, PARTS, input_step, 0)
 
     for copy in x_out + gz_out:
         copy.wait_send()

time: 207 us -> 179 us (0.86)
  the two profiles are of different devices: /device:TPU:106 before, /device:TPU:2 now
where the time goes in v2:
time: 179 us; the launch traced here: 178 us
  Pallas kernels  163 us (91%)
  local copies, waits for them, and re-layouts  15 us (8%)
    pallas_call x1, Pallas kernels, on_device(): pl.pallas_call(functools.partial(section_kernel, sections), out_shape=(ja...  163 us
    another operation x2, local copies, waits for them, and re-layouts, on_device(): return (grad[None], mantissa[None], scale[None])  7.57 us
    unnamed x5, local copies, waits for them, and re-layouts  7.39 us

profile of v2, /device:TPU:2, one launch (start us, length us, event | category | flops | bytes accessed | tf_op | source)
XLA Modules:
  0.0 178.3 jit_solution(4472603013348674418)
XLA Ops:
  0.6 1.0 copy.6
  1.6 0.0 copy-start
  1.6 5.1 %copy.7 = bf16[512,8,2,256]{3,1,2,0:T(8,128)(2,1)} copy(bf16[512,8,2,256]{3,2,1,0:T(2,128)(2,1)} %bitcast.16) | data formatting | bytes 8388608
  6.7 0.0 copy-done
  6.7 162.6 %section.1 = (bf16[1024,1024]{1,0:T(8,128)(2,1)S(1)}, bf16[4096,512]{1,0:T(8,128)(2,1)}, f32[8,4096]{1,0:T(8,128)S(1)}) custom-call(bf16[256,4096]{1,0:T(8,128)(2,1)S(1)} %bitcast.12, bf16[256,512]{1,0:T(8,128)(2,1)S(1)} %bitcast.14, bf16[4096,512]{1,0:T(8,128)(2,1)} %bitcast.15), custom_call_target="tpu_custom_call" | custom-call | tf_op jit(solution)/shard_map/section/pallas_call | solution.py:363
  169.4 0.7 broadcast_in_dim_reshape.7
  170.1 6.9 %broadcast_in_dim_reshape.6 = bf16[1,4096,2,256]{3,2,1,0:T(2,128)(2,1)} reshape(bf16[4096,512]{1,0:T(8,128)(2,1)} %get-tuple-element.7) | data formatting | bytes 8388608 | tf_op jit(solution)/shard_map/broadcast_in_dim;reshape | solution.py:410
  176.9 1.3 copy.9
  (1 shorter events, 0.0 us)
Async XLA Ops:
  1.6 5.1 %copy-start = (bf16[1,256,4096]{2,1,0:T(8,128)(2,1)S(1)}, bf16[1,256,4096]{2,1,0:T(8,128)(2,1)}, u32[]{:S(2)}) copy-start(bf16[1,256,4096]{2,1,0:T(8,128)(2,1)} %param.3) | copy-start | bytes 6291460

commit v3 on v2

--- a/solution.py
+++ b/solution.py
@@ -8,6 +8,8 @@
 from jax.sharding import PartitionSpec as P
 
 BLOCK = 128
+SIDE = 256
+EARLY = 3
 TINY = 1e-6
 MESH = pl.DeviceIdType.MESH
 PARTS = 4
@@ -27,6 +29,12 @@
     out_scale,
     x_stage,
     x_all,
+    g_raw,
+    g_own,
+    w_raw,
+    w_own,
+    spread,
+    gather,
     g_all,
     w_all,
     mant,
@@ -43,6 +51,10 @@
     gy_recv,
     gf_send,
     gf_recv,
+    gl_send,
+    gl_recv,
+    gn_send,
+    gn_recv,
     w_send,
     w_recv,
     m_send,
@@ -57,12 +69,13 @@
 ):
     pipe, dp, mp = lax.axis_index("pipe"), lax.axis_index("dp"), lax.axis_index("mp")
     tokens, features = x_ref.shape
-    columns = g_ref.shape[1]
+    columns = g_own.shape[1]
     share = features // PARTS
     chunk = share // PARTS
-    all_tokens = tokens * PARTS
-    half = all_tokens // 2
+    lead = tokens * 3 // 4
+    first, last = pl.ds(0, lead), pl.ds(lead, tokens - lead)
     blocks = columns // BLOCK
+    step = SIDE // blocks
 
     def along_mp(by):
         return (pipe, dp, wrap(mp + by))
@@ -75,6 +88,11 @@
             src_ref=src, dst_ref=dst, send_sem=send, recv_sem=recv, device_id=device, device_id_type=MESH
         )
 
+    g_in = pltpu.make_async_copy(g_ref, g_raw, local_sem.at[4])
+    w_in = pltpu.make_async_copy(w_ref, w_raw, local_sem.at[5])
+    g_in.start()
+    w_in.start()
+
     barrier = pltpu.get_barrier_semaphore()
     for by in range(1, PARTS):
         pl.semaphore_signal(barrier, inc=1, device_id=along_mp(by), device_id_type=MESH)
@@ -84,13 +102,33 @@
         pl.semaphore_signal(
             barrier, inc=1, device_id=(lax.rem(pipe + by, sections), dp, mp), device_id_type=MESH
         )
+
+    line = lax.broadcasted_iota(jnp.int32, (SIDE, SIDE), 0)
+    column = lax.broadcasted_iota(jnp.int32, (SIDE, SIDE), 1)
+
+    def place(index):
+        return (index % 2 * 2 + index // 2 % 2) * step + index // blocks
+
+    spread[...] = jnp.where(column == place(line), 1.0, 0.0).astype(jnp.bfloat16)
+    gather[...] = jnp.where(line == place(column), 1.0, 0.0).astype(jnp.bfloat16)
+
+    def untangle(raw, own, index):
+        many = pl.ds(pl.multiple_of(index * SIDE, SIDE), SIDE)
+        rows = pl.ds(pl.multiple_of(index * step, step), step)
+        sorted_rows = jnp.dot(gather[...], raw[many, :], preferred_element_type=jnp.float32)
+        for block in range(blocks):
+            own[rows, block * BLOCK : (block + 1) * BLOCK] = sorted_rows[
+                block * step : (block + 1) * step
+            ].astype(jnp.bfloat16)
+
+    g_in.wait()
+    for index in range(tokens // step):
+        untangle(g_raw, g_own, index)
+
     pl.semaphore_wait(barrier, 2 * (PARTS - 1) + 2)
 
     def quarter(index):
         return pl.ds(pl.multiple_of(index * share, share), share)
-
-    def token_rows(index):
-        return pl.ds(pl.multiple_of(index * tokens, tokens), tokens)
 
     x_out = [
         remote(
@@ -98,19 +136,44 @@
         )
         for by in range(1, PARTS)
     ]
+    gl_out = [
+        remote(g_own.at[last], g_all.at[by, dp, last], gl_send.at[by], gl_recv.at[by], along_mp(by))
+        for by in range(1, PARTS)
+    ]
+
+    def gn_copy(by, block):
+        part = g_all.at[:, block, last]
+        return remote(part, part, gn_send.at[by], gn_recv.at[by], along_dp(wrap(dp + by)))
+
+    for copy in gl_out:
+        copy.start()
     for copy in x_out:
         copy.start()
-    own_g = pltpu.make_async_copy(g_ref, g_all.at[0, token_rows(dp)], local_sem.at[0])
-    own_w = pltpu.make_async_copy(w_ref.at[quarter(mp)], w_all.at[0], local_sem.at[1])
+    own_g = pltpu.make_async_copy(g_own, g_all.at[0, dp], local_sem.at[0])
+    own_w = pltpu.make_async_copy(w_own.at[quarter(mp)], w_all.at[0], local_sem.at[1])
     own_g.start()
     gz_out = [
         remote(
-            g_ref, g_all.at[0, token_rows(dp)], gz_send.at[by], gz_recv.at[by], along_dp(wrap(dp + by))
+            g_own.at[first], g_all.at[0, dp, first], gz_send.at[by], gz_recv.at[by], along_dp(wrap(dp + by))
         )
         for by in range(1, PARTS)
     ]
     for copy in gz_out:
         copy.start()
+
+    own_g.wait()
+    for copy in gl_out:
+        copy.wait_recv()
+    for by in range(1, PARTS):
+        gn_copy(by, dp).start()
+    w_in.wait()
+
+    def untangle_weights(index, _):
+        for part in range(PARTS):
+            untangle(w_raw, w_own, index * PARTS + part)
+        return 0
+
+    lax.fori_loop(0, share // step, untangle_weights, 0)
     own_w.start()
 
     def x_from(by):
@@ -135,25 +198,24 @@
     def w_out(by, part):
         rows = pl.ds(pl.multiple_of(wrap(mp + by) * share + part * chunk, chunk), chunk)
         return remote(
-            w_ref.at[rows],
+            w_own.at[rows],
             w_all.at[by, pl.ds(pl.multiple_of(part * chunk, chunk), chunk)],
             w_send.at[by, part],
             w_recv.at[by, part],
             along_mp(by),
         )
 
-    for part in range(PARTS // 2):
+    for part in range(EARLY):
         for by in range(1, PARTS):
             w_out(by, part).start()
 
-    own_g.wait()
     for by in range(1, PARTS):
         remote(
-            g_ref, g_all.at[0, token_rows(wrap(dp - by))], gz_send.at[by], gz_recv.at[by], along_dp(wrap(dp + by))
+            g_own.at[first], g_all.at[0, wrap(dp - by), first], gz_send.at[by], gz_recv.at[by], along_dp(wrap(dp + by))
         ).wait_recv()
 
     def g_half(slot, part):
-        return g_all.at[slot, pl.ds(part * half, half)]
+        return g_all.at[slot, pl.ds(part * (PARTS // 2), PARTS // 2), first]
 
     def g_out(side, part):
         by, slot = (1, 1) if side == 0 else (-1, 3)
@@ -172,7 +234,7 @@
     for side in range(2):
         g_out(side, side).wait_recv()
         g_on(side).start()
-    for part in range(PARTS // 2, PARTS):
+    for part in range(EARLY, PARTS):
         for by in range(1, PARTS):
             w_out(by, part).start()
 
@@ -187,6 +249,8 @@
     for side in range(2):
         g_out(side, 1 - side).wait_recv()
         g_on(side).wait_recv()
+    for by in range(1, PARTS):
+        gn_copy(by, wrap(dp - by)).wait_recv()
     def p_out(part):
         cols = pl.ds(pl.multiple_of(part * chunk, chunk), chunk)
         before = jnp.maximum(pipe - 1, 0)
@@ -206,7 +270,7 @@
             total = None
             for slot in range(PARTS):
                 term = lax.dot_general(
-                    g_all[slot, own, :],
+                    g_all[slot, group],
                     w_all[slot, rows, :],
                     (((1,), (1,)), ((), ())),
                     preferred_element_type=jnp.float32,
@@ -230,24 +294,27 @@
         remote(x_stage.at[0], x_all.at[source], xz_send.at[0], xz_recv.at[source], along_dp(source)).wait_recv()
     pltpu.make_async_copy(x_stage.at[0], x_all.at[dp], local_sem.at[2]).wait()
 
+    def wide(first, size):
+        return pl.ds(pl.multiple_of(first * blocks, size * blocks), size * blocks)
+
     def m_out(turn, part):
-        rows = pl.ds(pl.multiple_of(mp * share + part * chunk, chunk), chunk)
-        src = mant.at[turn, pl.ds(pl.multiple_of(part * chunk, chunk), chunk)]
+        rows = wide(mp * share + part * chunk, chunk)
+        src = mant.at[turn, wide(part * chunk, chunk)]
         return remote(src, out_mant.at[rows], m_send.at[turn, part], m_recv.at[turn, part], along_mp(1 + turn))
 
     def m_here(part):
-        rows = pl.ds(pl.multiple_of(mp * share + part * chunk, chunk), chunk)
-        src = mant.at[PARTS - 1, pl.ds(pl.multiple_of(part * chunk, chunk), chunk)]
+        rows = wide(mp * share + part * chunk, chunk)
+        src = mant.at[PARTS - 1, wide(part * chunk, chunk)]
         return pltpu.make_async_copy(src, out_mant.at[rows], m_local.at[part])
 
-    def weight_step(step, _):
-        turn, part = step // PARTS, lax.rem(step, PARTS)
+    def weight_step(count, _):
+        turn, part = count // PARTS, lax.rem(count, PARTS)
         slot = PARTS - 1 - turn
         rows = pl.ds(pl.multiple_of(part * chunk, chunk), chunk)
         partial = [
             lax.dot_general(
                 x_all[group, :, rows],
-                g_all[slot, pl.ds(group * tokens, tokens), :],
+                g_all[slot, group],
                 (((0,), (0,)), ((), ())),
                 preferred_element_type=jnp.float32,
             )
@@ -258,6 +325,7 @@
             largest = jnp.maximum(largest, jnp.abs(partial[group]))
         lanes = lax.broadcasted_iota(jnp.int32, (chunk, BLOCK), 1)
         gathered = jnp.zeros((chunk, BLOCK), jnp.float32)
+        sums = []
         for block in range(blocks):
             cols = slice(block * BLOCK, (block + 1) * BLOCK)
             size = jnp.max(largest[:, cols], axis=1, keepdims=True) + TINY
@@ -267,7 +335,11 @@
             for group in range(PARTS):
                 term = (partial[group][:, cols] * inverse).astype(jnp.bfloat16).astype(jnp.float32)
                 total = term if total is None else total + term
-            mant[turn, rows, cols] = total.astype(jnp.bfloat16)
+            sums.append(total.astype(jnp.bfloat16))
+        for piece in range(chunk // step):
+            stacked = jnp.concatenate([one[piece * step : (piece + 1) * step] for one in sums], axis=0)
+            mixed = jnp.dot(spread[...], stacked, preferred_element_type=jnp.float32)
+            mant[turn, wide(part * chunk + piece * step, step), :] = mixed.astype(jnp.bfloat16)
         scale[turn, :, rows] = jnp.transpose(gathered)[:8, :]
 
         @pl.when(turn < PARTS - 1)
@@ -295,8 +367,10 @@
 
     lax.fori_loop(PARTS // 2, PARTS, input_step, 0)
 
-    for copy in x_out + gz_out:
+    for copy in x_out + gz_out + gl_out:
         copy.wait_send()
+    for by in range(1, PARTS):
+        gn_copy(by, dp).wait_send()
     for by in range(PARTS):
 
         @pl.when(wrap(mp - by) != dp)
@@ -314,9 +388,9 @@
         source = wrap(mp - 1 - turn)
         for part in range(PARTS):
             m_out(turn, part).wait_send()
-            rows = pl.ds(pl.multiple_of(source * share + part * chunk, chunk), chunk)
+            rows = wide(source * share + part * chunk, chunk)
             remote(
-                mant.at[turn, pl.ds(part * chunk, chunk)],
+                mant.at[turn, wide(part * chunk, chunk)],
                 out_mant.at[rows],
                 m_send.at[turn, part],
                 m_recv.at[turn, part],
@@ -349,13 +423,19 @@
             ).wait()
 
 
+def paired(array):
+    count, pair, columns = array.shape
+    split = array.reshape(count, pair, columns // BLOCK, BLOCK)
+    return split.transpose(0, 2, 1, 3).reshape(-1, BLOCK)
+
+
 def on_device(sections, layer_input, kv_cotangent, kv_weight):
     features = layer_input[0]
     tokens, width = features.shape
     columns = 2 * kv_cotangent.shape[3]
     rows = kv_weight.shape[1]
-    flat_grad = kv_cotangent.reshape(tokens, columns)
-    flat_weight = kv_weight.reshape(rows, columns)
+    flat_grad = paired(kv_cotangent[0])
+    flat_weight = paired(kv_weight[0])
     share = width // PARTS
     blocks = columns // BLOCK
     dma = pltpu.SemaphoreType.DMA
@@ -364,7 +444,7 @@
         functools.partial(section_kernel, sections),
         out_shape=(
             jax.ShapeDtypeStruct((tokens * PARTS, share), jnp.bfloat16),
-            jax.ShapeDtypeStruct((rows, columns), jnp.bfloat16),
+            jax.ShapeDtypeStruct((rows * blocks, BLOCK), jnp.bfloat16),
             jax.ShapeDtypeStruct((8, rows), jnp.float32),
         ),
         in_specs=[anywhere] * 3,
@@ -372,9 +452,15 @@
         scratch_shapes=[
             pltpu.VMEM((PARTS, tokens, share), jnp.bfloat16),
             pltpu.VMEM((PARTS, tokens, share), jnp.bfloat16),
-            pltpu.VMEM((PARTS, tokens * PARTS, columns), jnp.bfloat16),
+            pltpu.VMEM((tokens * blocks, BLOCK), jnp.bfloat16),
+            pltpu.VMEM((tokens, columns), jnp.bfloat16),
+            pltpu.VMEM((rows * blocks, BLOCK), jnp.bfloat16),
+            pltpu.VMEM((rows, columns), jnp.bfloat16),
+            pltpu.VMEM((SIDE, SIDE), jnp.bfloat16),
+            pltpu.VMEM((SIDE, SIDE), jnp.bfloat16),
+            pltpu.VMEM((PARTS, PARTS, tokens, columns), jnp.bfloat16),
             pltpu.VMEM((PARTS, share, columns), jnp.bfloat16),
-            pltpu.VMEM((PARTS, share, columns), jnp.bfloat16),
+            pltpu.VMEM((PARTS, share * blocks, BLOCK), jnp.bfloat16),
             pltpu.VMEM((PARTS, 8, share), jnp.float32),
             pltpu.VMEM((tokens * PARTS, share), jnp.bfloat16),
             pltpu.VMEM((tokens, share), jnp.bfloat16),
@@ -388,6 +474,10 @@
             dma((2, 2)),
             dma((2,)),
             dma((2,)),
+            dma((PARTS,)),
+            dma((PARTS,)),
+            dma((PARTS,)),
+            dma((PARTS,)),
             dma((PARTS, PARTS)),
             dma((PARTS, PARTS)),
             dma((PARTS, PARTS)),
@@ -396,15 +486,16 @@
             dma((PARTS,)),
             dma((PARTS,)),
             dma((PARTS,)),
-            dma((4,)),
+            dma((6,)),
             dma((PARTS,)),
             dma((PARTS,)),
         ],
         name="section",
         compiler_params=pltpu.CompilerParams(
-            collective_id=0, has_side_effects=True, vmem_limit_bytes=48 << 20
+            collective_id=0, has_side_effects=True, vmem_limit_bytes=56 << 20
         ),
     )(features, flat_grad, flat_weight)
+    mantissa = mantissa.reshape(rows, blocks // 2, 2, BLOCK).transpose(0, 2, 1, 3)
     mantissa = mantissa.reshape(rows, 2, columns // 2)
     scale = scale[:blocks].T.reshape(rows, 2, blocks // 2)
     return grad[None], mantissa[None], scale[None]

time: 179 us -> 165 us (0.922)
  local copies, waits for them, and re-layouts: 15 us -> 6.85 us
  Pallas kernels: 163 us -> 157 us
    another operation x2 -> x1, local copies, waits for them, and re-layouts: 7.57 us -> 0.68 us  [on_device(): return (grad[None], mantissa[None], scale[None])]
    pallas_call x1, Pallas kernels: 163 us -> 157 us  [on_device(): pl.pallas_call(functools.partial(section_kernel, sections), out_shape=(ja...]
    unnamed x5 -> x4, local copies, waits for them, and re-layouts: 7.39 us -> 5.25 us
where the time goes in v3:
time: 165 us
  Pallas kernels  157 us (95%)
  local copies, waits for them, and re-layouts  6.85 us (4%)
    pallas_call x1, Pallas kernels, on_device(): pl.pallas_call(functools.partial(section_kernel, sections), out_shape=(ja...  157 us
    unnamed x4, local copies, waits for them, and re-layouts  5.25 us

profile of v3, /device:TPU:2, one launch (start us, length us, event | category | flops | bytes accessed | tf_op | source)
XLA Modules:
  0.0 164.9 jit_solution(7695164986297230586)
XLA Ops:
  0.6 157.4 %section.1 = (bf16[1024,1024]{1,0:T(8,128)(2,1)}, bf16[16384,128]{1,0:T(8,128)(2,1)}, f32[8,4096]{1,0:T(8,128)}) custom-call(bf16[256,4096]{1,0:T(8,128)(2,1)} %bitcast.23, bf16[1024,128]{1,0:T(8,128)(2,1)} %bitcast.25, bf16[16384,128]{1,0:T(8,128)(2,1)} %bitcast.21), custom_call_target="tpu_custom_call" | custom-call | tf_op jit(solution)/shard_map/section/pallas_call | solution.py:443
  158.0 0.9 slice_bitcast_fusion
  158.9 0.7 broadcast_in_dim_reshape.7
  159.6 0.0 copy-start
  159.6 3.2 %copy.11 = bf16[1,1024,1024]{2,1,0:T(8,128)(2,1)} copy(bf16[1,1024,1024]{2,1,0:T(8,128)(2,1)} %bitcast.24) | data formatting | bytes 4194304
  162.8 0.0 copy-done
  162.9 2.0 %copy.12 = bf16[1,4096,2,256]{3,2,1,0:T(2,128)(2,1)} copy(bf16[1,4096,2,256]{3,2,1,0:T(2,128)(2,1)S(1)} %bitcast.22) | data formatting | bytes 8388608
Async XLA Ops:
  159.6 3.2 %copy-start = (bf16[16384,128]{1,0:T(8,128)(2,1)S(1)}, bf16[16384,128]{1,0:T(8,128)(2,1)}, u32[]{:S(2)}) copy-start(bf16[16384,128]{1,0:T(8,128)(2,1)} %get-tuple-element.7) | copy-start | bytes 12582916

commit v4 on v3

--- a/solution.py
+++ b/solution.py
@@ -30,7 +30,6 @@
     x_stage,
     x_all,
     g_raw,
-    g_own,
     w_raw,
     w_own,
     spread,
@@ -69,10 +68,10 @@
 ):
     pipe, dp, mp = lax.axis_index("pipe"), lax.axis_index("dp"), lax.axis_index("mp")
     tokens, features = x_ref.shape
-    columns = g_own.shape[1]
+    columns = g_all.shape[3]
     share = features // PARTS
     chunk = share // PARTS
-    lead = tokens * 3 // 4
+    lead = tokens // 2
     first, last = pl.ds(0, lead), pl.ds(lead, tokens - lead)
     blocks = columns // BLOCK
     step = SIDE // blocks
@@ -123,7 +122,7 @@
 
     g_in.wait()
     for index in range(tokens // step):
-        untangle(g_raw, g_own, index)
+        untangle(g_raw, g_all.at[0, dp], index)
 
     pl.semaphore_wait(barrier, 2 * (PARTS - 1) + 2)
 
@@ -137,35 +136,57 @@
         for by in range(1, PARTS)
     ]
     gl_out = [
-        remote(g_own.at[last], g_all.at[by, dp, last], gl_send.at[by], gl_recv.at[by], along_mp(by))
+        remote(
+            g_all.at[0, dp, last], g_all.at[by, dp, last], gl_send.at[by], gl_recv.at[by], along_mp(by)
+        )
         for by in range(1, PARTS)
     ]
-
-    def gn_copy(by, block):
-        part = g_all.at[:, block, last]
-        return remote(part, part, gn_send.at[by], gn_recv.at[by], along_dp(wrap(dp + by)))
+    GZ, GN = 0, 1
+
+    def block_of(side, back):
+        return wrap(dp - back if side == 0 else dp + back)
+
+    def chain(kind, side, turn, back):
+        block = block_of(side, back)
+        part = g_all.at[0, block, first] if kind == GZ else g_all.at[:, block, last]
+        send, recv = (gz_send, gz_recv) if kind == GZ else (gn_send, gn_recv)
+        return remote(part, part, send.at[side, turn], recv.at[side, turn], along_dp(block_of(side, -1)))
+
+    def goes(side, turn):
+        if side == 0:
+            return jnp.logical_and(dp >= turn, dp < PARTS - 1)
+        return jnp.logical_and(dp + turn < PARTS, dp > 0)
+
+    def comes(side, turn):
+        return dp > turn if side == 0 else dp + turn < PARTS - 1
+
+    def hop(kind, side, turn):
+        @pl.when(goes(side, turn))
+        def _():
+            chain(kind, side, turn, turn).start()
+
+    def arrive(kind, side, turn):
+        @pl.when(comes(side, turn))
+        def _():
+            chain(kind, side, turn, turn + 1).wait_recv()
+
+    def pass_on(kind, turn):
+        for side in range(2):
+            arrive(kind, side, turn)
+            if turn + 1 < PARTS - 1:
+                hop(kind, side, turn + 1)
 
     for copy in gl_out:
         copy.start()
+    for side in range(2):
+        hop(GZ, side, 0)
     for copy in x_out:
         copy.start()
-    own_g = pltpu.make_async_copy(g_own, g_all.at[0, dp], local_sem.at[0])
     own_w = pltpu.make_async_copy(w_own.at[quarter(mp)], w_all.at[0], local_sem.at[1])
-    own_g.start()
-    gz_out = [
-        remote(
-            g_own.at[first], g_all.at[0, dp, first], gz_send.at[by], gz_recv.at[by], along_dp(wrap(dp + by))
-        )
-        for by in range(1, PARTS)
-    ]
-    for copy in gz_out:
-        copy.start()
-
-    own_g.wait()
     for copy in gl_out:
         copy.wait_recv()
-    for by in range(1, PARTS):
-        gn_copy(by, dp).start()
+    for side in range(2):
+        hop(GN, side, 0)
     w_in.wait()
 
     def untangle_weights(index, _):
@@ -175,6 +196,8 @@
 
     lax.fori_loop(0, share // step, untangle_weights, 0)
     own_w.start()
+    pass_on(GZ, 0)
+    pass_on(GN, 0)
 
     def x_from(by):
         return x_ref.at[:, quarter(mp)] if by == 0 else x_stage.at[by]
@@ -183,17 +206,8 @@
         owner = wrap(mp - by)
         return remote(x_from(by), x_all.at[dp], xz_send.at[by], xz_recv.at[dp], along_dp(owner))
 
-    for by in range(PARTS):
-        if by > 0:
-            x_out[by - 1].wait_recv()
-
-        @pl.when(wrap(mp - by) != dp)
-        def _():
-            x_on(by).start()
-
-        @pl.when(wrap(mp - by) == dp)
-        def _():
-            pltpu.make_async_copy(x_from(by), x_all.at[dp], local_sem.at[2]).start()
+    for copy in x_out:
+        copy.wait_recv()
 
     def w_out(by, part):
         rows = pl.ds(pl.multiple_of(wrap(mp + by) * share + part * chunk, chunk), chunk)
@@ -209,10 +223,18 @@
         for by in range(1, PARTS):
             w_out(by, part).start()
 
-    for by in range(1, PARTS):
-        remote(
-            g_own.at[first], g_all.at[0, wrap(dp - by), first], gz_send.at[by], gz_recv.at[by], along_dp(wrap(dp + by))
-        ).wait_recv()
+    pass_on(GZ, 1)
+    pass_on(GN, 1)
+    for by in range(PARTS):
+        @pl.when(wrap(mp - by) != dp)
+        def _():
+            x_on(by).start()
+
+        @pl.when(wrap(mp - by) == dp)
+        def _():
+            pltpu.make_async_copy(x_from(by), x_all.at[dp], local_sem.at[2]).start()
+
+    pass_on(GZ, 2)
 
     def g_half(slot, part):
         return g_all.at[slot, pl.ds(part * (PARTS // 2), PARTS // 2), first]
@@ -249,8 +271,7 @@
     for side in range(2):
         g_out(side, 1 - side).wait_recv()
         g_on(side).wait_recv()
-    for by in range(1, PARTS):
-        gn_copy(by, wrap(dp - by)).wait_recv()
+    pass_on(GN, 2)
     def p_out(part):
         cols = pl.ds(pl.multiple_of(part * chunk, chunk), chunk)
         before = jnp.maximum(pipe - 1, 0)
@@ -287,7 +308,7 @@
 
         return 0
 
-    lax.fori_loop(0, PARTS // 2, input_step, 0)
+    lax.fori_loop(0, EARLY, input_step, 0)
 
     for by in range(1, PARTS):
         source = wrap(dp - by)
@@ -340,7 +361,9 @@
             stacked = jnp.concatenate([one[piece * step : (piece + 1) * step] for one in sums], axis=0)
             mixed = jnp.dot(spread[...], stacked, preferred_element_type=jnp.float32)
             mant[turn, wide(part * chunk + piece * step, step), :] = mixed.astype(jnp.bfloat16)
-        scale[turn, :, rows] = jnp.transpose(gathered)[:8, :]
+        turned = jnp.transpose(gathered)
+        for kind in range(2):
+            scale[turn, kind, :, rows] = turned[kind * (blocks // 2) : (kind + 1) * (blocks // 2), :]
 
         @pl.when(turn < PARTS - 1)
         def _():
@@ -356,21 +379,27 @@
 
     def s_out(turn):
         cols = pl.ds(pl.multiple_of(mp * share, share), share)
-        return remote(scale.at[turn], out_scale.at[:, cols], s_send.at[turn], s_recv.at[turn], along_mp(1 + turn))
+        return remote(scale.at[turn], out_scale.at[:, :, cols], s_send.at[turn], s_recv.at[turn], along_mp(1 + turn))
 
     for turn in range(PARTS - 1):
         s_out(turn).start()
     s_here = pltpu.make_async_copy(
-        scale.at[PARTS - 1], out_scale.at[:, pl.ds(pl.multiple_of(mp * share, share), share)], local_sem.at[3]
+        scale.at[PARTS - 1], out_scale.at[:, :, pl.ds(pl.multiple_of(mp * share, share), share)], local_sem.at[3]
     )
     s_here.start()
 
-    lax.fori_loop(PARTS // 2, PARTS, input_step, 0)
-
-    for copy in x_out + gz_out + gl_out:
+    lax.fori_loop(EARLY, PARTS, input_step, 0)
+
+    for copy in x_out + gl_out:
         copy.wait_send()
-    for by in range(1, PARTS):
-        gn_copy(by, dp).wait_send()
+    for kind in (GZ, GN):
+        for side in range(2):
+            for turn in range(PARTS - 1):
+
+                @pl.when(goes(side, turn))
+                def _():
+                    chain(kind, side, turn, turn).wait_send()
+
     for by in range(PARTS):
 
         @pl.when(wrap(mp - by) != dp)
@@ -399,7 +428,7 @@
         s_out(turn).wait_send()
         cols = pl.ds(pl.multiple_of(source * share, share), share)
         remote(
-            scale.at[turn], out_scale.at[:, cols], s_send.at[turn], s_recv.at[turn], along_mp(1 + turn)
+            scale.at[turn], out_scale.at[:, :, cols], s_send.at[turn], s_recv.at[turn], along_mp(1 + turn)
         ).wait_recv()
     for part in range(PARTS):
         m_here(part).wait()
@@ -445,7 +474,7 @@
         out_shape=(
             jax.ShapeDtypeStruct((tokens * PARTS, share), jnp.bfloat16),
             jax.ShapeDtypeStruct((rows * blocks, BLOCK), jnp.bfloat16),
-            jax.ShapeDtypeStruct((8, rows), jnp.float32),
+            jax.ShapeDtypeStruct((2, blocks // 2, rows), jnp.float32),
         ),
         in_specs=[anywhere] * 3,
         out_specs=[anywhere] * 3,
@@ -453,7 +482,6 @@
             pltpu.VMEM((PARTS, tokens, share), jnp.bfloat16),
             pltpu.VMEM((PARTS, tokens, share), jnp.bfloat16),
             pltpu.VMEM((tokens * blocks, BLOCK), jnp.bfloat16),
-            pltpu.VMEM((tokens, columns), jnp.bfloat16),
             pltpu.VMEM((rows * blocks, BLOCK), jnp.bfloat16),
             pltpu.VMEM((rows, columns), jnp.bfloat16),
             pltpu.VMEM((SIDE, SIDE), jnp.bfloat16),
@@ -461,23 +489,23 @@
             pltpu.VMEM((PARTS, PARTS, tokens, columns), jnp.bfloat16),
             pltpu.VMEM((PARTS, share, columns), jnp.bfloat16),
             pltpu.VMEM((PARTS, share * blocks, BLOCK), jnp.bfloat16),
-            pltpu.VMEM((PARTS, 8, share), jnp.float32),
+            pltpu.VMEM((PARTS, 2, blocks // 2, share), jnp.float32),
             pltpu.VMEM((tokens * PARTS, share), jnp.bfloat16),
             pltpu.VMEM((tokens, share), jnp.bfloat16),
             dma((PARTS,)),
             dma((PARTS,)),
             dma((PARTS,)),
             dma((PARTS,)),
-            dma((PARTS,)),
-            dma((PARTS,)),
+            dma((2, PARTS)),
+            dma((2, PARTS)),
             dma((2, 2)),
             dma((2, 2)),
             dma((2,)),
             dma((2,)),
             dma((PARTS,)),
             dma((PARTS,)),
-            dma((PARTS,)),
-            dma((PARTS,)),
+            dma((2, PARTS)),
+            dma((2, PARTS)),
             dma((PARTS, PARTS)),
             dma((PARTS, PARTS)),
             dma((PARTS, PARTS)),
@@ -497,7 +525,7 @@
     )(features, flat_grad, flat_weight)
     mantissa = mantissa.reshape(rows, blocks // 2, 2, BLOCK).transpose(0, 2, 1, 3)
     mantissa = mantissa.reshape(rows, 2, columns // 2)
-    scale = scale[:blocks].T.reshape(rows, 2, blocks // 2)
+    scale = scale.transpose(2, 0, 1)
     return grad[None], mantissa[None], scale[None]
 
 

time: 165 us -> 159 us (0.964)
  Pallas kernels: 157 us -> 152 us
    pallas_call x1, Pallas kernels: 157 us -> 152 us  [on_device(): pl.pallas_call(functools.partial(section_kernel, sections), out_shape=(ja...]
    unnamed x4 -> x7, local copies, waits for them, and re-layouts: 5.25 us -> 5.89 us
where the time goes in v4:
time: 159 us; the launch traced here: 158 us
  Pallas kernels  152 us (96%)
  local copies, waits for them, and re-layouts  5.89 us (4%)
    pallas_call x1, Pallas kernels, on_device(): pl.pallas_call(functools.partial(section_kernel, sections), out_shape=(ja...  152 us
    unnamed x7, local copies, waits for them, and re-layouts  5.89 us

profile of v4, /device:TPU:2, one launch (start us, length us, event | category | flops | bytes accessed | tf_op | source)
XLA Modules:
  0.0 158.4 jit_solution(9708482044622158716)
XLA Ops:
  0.6 151.8 %section.1 = (bf16[1024,1024]{1,0:T(8,128)(2,1)}, bf16[16384,128]{1,0:T(8,128)(2,1)}, f32[2,2,4096]{2,1,0:T(2,128)}) custom-call(bf16[256,4096]{1,0:T(8,128)(2,1)} %bitcast.22, bf16[1024,128]{1,0:T(8,128)(2,1)} %bitcast.24, bf16[16384,128]{1,0:T(8,128)(2,1)} %bitcast.20), custom_call_target="tpu_custom_call" | custom-call | tf_op jit(solution)/shard_map/section/pallas_call | solution.py:472
  152.5 0.0 copy-start
  152.5 3.2 %copy.12 = bf16[1,1024,1024]{2,1,0:T(8,128)(2,1)} copy(bf16[1,1024,1024]{2,1,0:T(8,128)(2,1)} %bitcast.23) | data formatting | bytes 4194304
  155.7 0.0 copy-done
  155.7 0.0 copy-start.1
  155.7 2.0 %copy.13 = bf16[1,4096,2,256]{3,2,1,0:T(2,128)(2,1)} copy(bf16[1,4096,2,256]{3,2,1,0:T(2,128)(2,1)S(1)} %bitcast.21) | data formatting | bytes 8388608
  157.7 0.0 copy-done.1
  157.7 0.6 copy.14
Async XLA Ops:
  152.5 3.2 %copy-start = (bf16[16384,128]{1,0:T(8,128)(2,1)S(1)}, bf16[16384,128]{1,0:T(8,128)(2,1)}, u32[]{:S(2)}) copy-start(bf16[16384,128]{1,0:T(8,128)(2,1)} %get-tuple-element.7) | copy-start | bytes 12582916
  155.7 2.0 %copy-start.1 = (f32[2,2,4096]{2,1,0:T(2,128)S(1)}, f32[2,2,4096]{2,1,0:T(2,128)}, u32[]{:S(2)}) copy-start(f32[2,2,4096]{2,1,0:T(2,128)} %get-tuple-element.8) | copy-start | bytes 196612

commit v5 on v4

--- a/solution.py
+++ b/solution.py
@@ -71,7 +71,7 @@
     columns = g_all.shape[3]
     share = features // PARTS
     chunk = share // PARTS
-    lead = tokens // 2
+    lead = tokens * 7 // 16
     first, last = pl.ds(0, lead), pl.ds(lead, tokens - lead)
     blocks = columns // BLOCK
     step = SIDE // blocks

time: 159 us -> 158 us (level)
  Pallas kernels: 152 us -> 150 us
where the time goes in v5:
time: 158 us; the launch traced here: 157 us
  Pallas kernels  150 us (95%)
  local copies, waits for them, and re-layouts  5.89 us (4%)
    pallas_call x1, Pallas kernels, on_device(): pl.pallas_call(functools.partial(section_kernel, sections), out_shape=(ja...  150 us
    unnamed x7, local copies, waits for them, and re-layouts  5.89 us

profile of v5, /device:TPU:2, one launch (start us, length us, event | category | flops | bytes accessed | tf_op | source)
XLA Modules:
  0.0 157.0 jit_solution(11137309703770544110)
XLA Ops:
  0.6 150.4 %section.1 = (bf16[1024,1024]{1,0:T(8,128)(2,1)}, bf16[16384,128]{1,0:T(8,128)(2,1)}, f32[2,2,4096]{2,1,0:T(2,128)}) custom-call(bf16[256,4096]{1,0:T(8,128)(2,1)} %bitcast.22, bf16[1024,128]{1,0:T(8,128)(2,1)} %bitcast.24, bf16[16384,128]{1,0:T(8,128)(2,1)} %bitcast.20), custom_call_target="tpu_custom_call" | custom-call | tf_op jit(solution)/shard_map/section/pallas_call | solution.py:472
  151.1 0.0 copy-start
  151.1 3.2 %copy.12 = bf16[1,1024,1024]{2,1,0:T(8,128)(2,1)} copy(bf16[1,1024,1024]{2,1,0:T(8,128)(2,1)} %bitcast.23) | data formatting | bytes 4194304
  154.3 0.0 copy-done
  154.3 0.0 copy-start.1
  154.3 2.0 %copy.13 = bf16[1,4096,2,256]{3,2,1,0:T(2,128)(2,1)} copy(bf16[1,4096,2,256]{3,2,1,0:T(2,128)(2,1)S(1)} %bitcast.21) | data formatting | bytes 8388608
  156.3 0.0 copy-done.1
  156.3 0.6 copy.14
Async XLA Ops:
  151.1 3.2 %copy-start = (bf16[16384,128]{1,0:T(8,128)(2,1)S(1)}, bf16[16384,128]{1,0:T(8,128)(2,1)}, u32[]{:S(2)}) copy-start(bf16[16384,128]{1,0:T(8,128)(2,1)} %get-tuple-element.7) | copy-start | bytes 12582916
  154.3 2.0 %copy-start.1 = (f32[2,2,4096]{2,1,0:T(2,128)S(1)}, f32[2,2,4096]{2,1,0:T(2,128)}, u32[]{:S(2)}) copy-start(f32[2,2,4096]{2,1,0:T(2,128)} %get-tuple-element.8) | copy-start | bytes 196612

commit v6 on v5

--- a/solution.py
+++ b/solution.py
@@ -315,13 +315,16 @@
         remote(x_stage.at[0], x_all.at[source], xz_send.at[0], xz_recv.at[source], along_dp(source)).wait_recv()
     pltpu.make_async_copy(x_stage.at[0], x_all.at[dp], local_sem.at[2]).wait()
 
+    def reach(turn):
+        return 2 - turn + 3 * (turn // 2) + 2 * (turn // 3)
+
     def wide(first, size):
         return pl.ds(pl.multiple_of(first * blocks, size * blocks), size * blocks)
 
     def m_out(turn, part):
         rows = wide(mp * share + part * chunk, chunk)
         src = mant.at[turn, wide(part * chunk, chunk)]
-        return remote(src, out_mant.at[rows], m_send.at[turn, part], m_recv.at[turn, part], along_mp(1 + turn))
+        return remote(src, out_mant.at[rows], m_send.at[turn, part], m_recv.at[turn, part], along_mp(reach(turn)))
 
     def m_here(part):
         rows = wide(mp * share + part * chunk, chunk)
@@ -330,7 +333,7 @@
 
     def weight_step(count, _):
         turn, part = count // PARTS, lax.rem(count, PARTS)
-        slot = PARTS - 1 - turn
+        slot = PARTS - reach(turn)
         rows = pl.ds(pl.multiple_of(part * chunk, chunk), chunk)
         partial = [
             lax.dot_general(
@@ -379,7 +382,7 @@
 
     def s_out(turn):
         cols = pl.ds(pl.multiple_of(mp * share, share), share)
-        return remote(scale.at[turn], out_scale.at[:, :, cols], s_send.at[turn], s_recv.at[turn], along_mp(1 + turn))
+        return remote(scale.at[turn], out_scale.at[:, :, cols], s_send.at[turn], s_recv.at[turn], along_mp(reach(turn)))
 
     for turn in range(PARTS - 1):
         s_out(turn).start()
@@ -414,7 +417,7 @@
         for part in range(PARTS):
             w_out(by, part).wait_send()
     for turn in range(PARTS - 1):
-        source = wrap(mp - 1 - turn)
+        source = wrap(mp - reach(turn))
         for part in range(PARTS):
             m_out(turn, part).wait_send()
             rows = wide(source * share + part * chunk, chunk)
@@ -423,12 +426,12 @@
                 out_mant.at[rows],
                 m_send.at[turn, part],
                 m_recv.at[turn, part],
-                along_mp(1 + turn),
+                along_mp(reach(turn)),
             ).wait_recv()
         s_out(turn).wait_send()
         cols = pl.ds(pl.multiple_of(source * share, share), share)
         remote(
-            scale.at[turn], out_scale.at[:, :, cols], s_send.at[turn], s_recv.at[turn], along_mp(1 + turn)
+            scale.at[turn], out_scale.at[:, :, cols], s_send.at[turn], s_recv.at[turn], along_mp(reach(turn))
         ).wait_recv()
     for part in range(PARTS):
         m_here(part).wait()

time: 158 us -> 156 us (0.987)
  no operation moved by 1% of the time
where the time goes in v6:
time: 156 us
  Pallas kernels  150 us (96%)
  local copies, waits for them, and re-layouts  5.89 us (4%)
    pallas_call x1, Pallas kernels, on_device(): pl.pallas_call(functools.partial(section_kernel, sections), out_shape=(ja...  150 us
    unnamed x7, local copies, waits for them, and re-layouts  5.89 us

profile of v6, /device:TPU:2, one launch (start us, length us, event | category | flops | bytes accessed | tf_op | source)
XLA Modules:
  0.0 156.3 jit_solution(11463558666819085167)
XLA Ops:
  0.6 149.7 %section.1 = (bf16[1024,1024]{1,0:T(8,128)(2,1)}, bf16[16384,128]{1,0:T(8,128)(2,1)}, f32[2,2,4096]{2,1,0:T(2,128)}) custom-call(bf16[256,4096]{1,0:T(8,128)(2,1)} %bitcast.22, bf16[1024,128]{1,0:T(8,128)(2,1)} %bitcast.24, bf16[16384,128]{1,0:T(8,128)(2,1)} %bitcast.20), custom_call_target="tpu_custom_call" | custom-call | tf_op jit(solution)/shard_map/section/pallas_call | solution.py:475
  150.4 0.0 copy-start
  150.4 3.2 %copy.12 = bf16[1,1024,1024]{2,1,0:T(8,128)(2,1)} copy(bf16[1,1024,1024]{2,1,0:T(8,128)(2,1)} %bitcast.23) | data formatting | bytes 4194304
  153.6 0.0 copy-done
  153.6 0.0 copy-start.1
  153.6 2.0 %copy.13 = bf16[1,4096,2,256]{3,2,1,0:T(2,128)(2,1)} copy(bf16[1,4096,2,256]{3,2,1,0:T(2,128)(2,1)S(1)} %bitcast.21) | data formatting | bytes 8388608
  155.6 0.0 copy-done.1
  155.6 0.6 copy.14
Async XLA Ops:
  150.4 3.2 %copy-start = (bf16[16384,128]{1,0:T(8,128)(2,1)S(1)}, bf16[16384,128]{1,0:T(8,128)(2,1)}, u32[]{:S(2)}) copy-start(bf16[16384,128]{1,0:T(8,128)(2,1)} %get-tuple-element.7) | copy-start | bytes 12582916
  153.6 2.0 %copy-start.1 = (f32[2,2,4096]{2,1,0:T(2,128)S(1)}, f32[2,2,4096]{2,1,0:T(2,128)}, u32[]{:S(2)}) copy-start(f32[2,2,4096]{2,1,0:T(2,128)} %get-tuple-element.8) | copy-start | bytes 196612
